TPU v7x, 32 devices: a whole 2x2x4 slice. The times are simulated.
32 devices in a mesh: seq: 8 (over y, x, core), fsdp: 4 (over z).
Axes of the slice: x: 2, y: 2, z: 4, core: 2. Of those that a mesh axis runs over, the one named last changes fastest.
Arguments:
- tokens: bfloat16 [4, 2048, 1536], P('fsdp', 'seq'), may hold values from -6 to 6
- segment_ids: int32 [4, 2048], P('fsdp'), may hold values from 0 to 7, never falling along the last dimension, each value on 1 to 512 neighbouring positions
- cotangent: bfloat16 [4, 2048, 1536], P('fsdp', 'seq'), may hold values from -6 to 6
- w_in: bfloat16 [1536, 6448], P('fsdp'), may hold values from -0.15625 to 0.15625
- w_out: bfloat16 [3072, 1536], P('fsdp'), may hold values from -0.109375 to 0.109375
- conv_w: bfloat16 [4, 3328], P(None, 'fsdp'), may hold values from -3 to 3
- conv_b: bfloat16 [3328], P('fsdp'), may hold values from -1.5 to 1.5
- a_log: bfloat16 [48], P('fsdp'), may hold values from -3 to 1.5
- dt_bias: bfloat16 [48], P('fsdp'), may hold values from -5.5 to -3
- d_skip: bfloat16 [48], P('fsdp'), may hold values from 0.5 to 1.5
- norm_w: bfloat16 [1536], P('fsdp'), may hold values from 0.5 to 1.5
- gate_w: bfloat16 [3072], P('fsdp'), may hold values from 0.5 to 1.5
Outputs:
- layer_out: bfloat16 [4, 2048, 1536], P('fsdp', 'seq')
- token_grad: float32 [4, 2048, 1536], P('fsdp', 'seq')
- w_in_grad: float32 [1536, 6448], P('fsdp')
- w_out_grad: float32 [3072, 1536], P('fsdp')
- conv_w_grad: float32 [4, 3328], P(None, 'fsdp')
- conv_b_grad: float32 [3328], P('fsdp')
- a_log_grad: float32 [48], P('fsdp')
- dt_bias_grad: float32 [48], P('fsdp')
- d_skip_grad: float32 [48], P('fsdp')
- norm_w_grad: float32 [1536], P('fsdp')
- gate_w_grad: float32 [3072], P('fsdp')
Inputs may be any that keep to these rules, and one draw needn't show every extreme that they name: `segment_ids`: in each sequence the ids never fall from one token to the next, start at 0 and take every value; each document has 1 to 512 tokens and one has exactly 512.
All inputs are finite; a program needn't handle non-finite values.
Results may differ from a plain program's by a relative error of at most 0.011.
Values may be sent and summed in bfloat16 or wider, within the bound.
A program may use at most 320 MiB of HBM per device.

v0:
```python
import jax
import jax.numpy as jnp
from jax import lax
from jax.sharding import PartitionSpec as P

DI = 3072
HEADDIM = 64
STATE = 128
CONV = 4
SPAN = 256
HEADS = 48
CHAN = 3328
EPSILON = 1e-05
HIGHEST = lax.Precision.HIGHEST


def passed_along(value, axis, steps):
    count = lax.axis_size(axis)
    first, last = (max(0, -steps), min(count, count - steps))
    return lax.ppermute(value, axis, [(source, source + steps) for source in range(first, last)])


def shortened(array):

    def short(part):
        return part.astype(jnp.bfloat16) if part.dtype == jnp.float32 else part

    return jax.tree.map(short, array)


def block_masks(ids_blocks, before_ids):
    block_len = ids_blocks.shape[1]
    places = jnp.arange(block_len)
    causal_mask = (places[:, None] >= places[None, :])[None] & (
        ids_blocks[:, :, None] == ids_blocks[:, None, :]
    )
    keep_flag = (ids_blocks == before_ids[:, None]).astype(jnp.float32)
    same_last = (ids_blocks == ids_blocks[:, -1:]).astype(jnp.float32)
    return (causal_mask, keep_flag, same_last)


def local_states(x_heads, b_rows, step_size, log_decay, same_last, keep_flag):
    cum_decay = jnp.cumsum(log_decay, axis=1)
    last_cum = cum_decay[:, -1]
    weights = jnp.exp(last_cum[:, None, :] - cum_decay) * step_size * same_last[:, :, None]
    fresh_state = jnp.einsum("csh,cshp,csn->chpn", weights, x_heads, b_rows, precision=HIGHEST)
    passing = keep_flag[:, -1:] * jnp.exp(last_cum)
    total_state = jnp.zeros_like(fresh_state[0])
    total_decay = jnp.ones_like(passing[0])
    total_state = fresh_state[0] + passing[0][:, None, None] * total_state
    total_decay = total_decay * passing[0]
    return (fresh_state, passing, total_state, total_decay)


def local_output(x_heads, b_rows, c_rows, step_size, log_decay, incoming, causal_mask, keep_flag):
    cum_decay = jnp.cumsum(log_decay, axis=1)
    cum_heads = jnp.swapaxes(cum_decay, 1, 2)
    gap_decay = cum_heads[:, :, :, None] - cum_heads[:, :, None, :]
    head_mask = causal_mask[:, None]
    decay_map = jnp.exp(jnp.where(head_mask, gap_decay, 0.0)) * head_mask.astype(jnp.float32)
    scores = jnp.einsum("ctn,csn->cts", c_rows, b_rows, precision=HIGHEST)
    mixing = scores[:, None] * decay_map * jnp.swapaxes(step_size, 1, 2)[:, :, None, :]
    inner_out = jnp.einsum("chts,cshp->cthp", mixing, x_heads, precision=HIGHEST)
    starts = [incoming]
    start_states = jnp.stack(starts)
    carried = jnp.einsum("ctn,chpn->cthp", c_rows, start_states, precision=HIGHEST)
    carried = carried * (keep_flag[:, :, None] * jnp.exp(cum_decay))[..., None]
    return inner_out + carried


def on_device(
    tokens,
    segment_ids,
    cotangent,
    w_in,
    w_out,
    conv_w,
    conv_b,
    a_log,
    dt_bias,
    d_skip,
    norm_w,
    gate_w,
):
    gathered = (
        lax.all_gather(w_in, "fsdp", axis=0, tiled=True),
        lax.all_gather(w_out, "fsdp", axis=0, tiled=True),
        lax.all_gather(conv_w, "fsdp", axis=1, tiled=True),
        lax.all_gather(conv_b, "fsdp", axis=0, tiled=True),
        lax.all_gather(a_log, "fsdp", axis=0, tiled=True),
        lax.all_gather(dt_bias, "fsdp", axis=0, tiled=True),
        lax.all_gather(d_skip, "fsdp", axis=0, tiled=True),
        lax.all_gather(norm_w, "fsdp", axis=0, tiled=True),
        lax.all_gather(gate_w, "fsdp", axis=0, tiled=True),
    )
    (
        w_in_full,
        w_out_full,
        conv_full,
        bias_full,
        a_log_full,
        dt_bias_full,
        skip_full,
        norm_full,
        gate_full,
    ) = gathered
    inputs = tokens[0].astype(jnp.float32)
    length = inputs.shape[0]
    norm_gain = norm_full.astype(jnp.float32)
    scale_in = lax.rsqrt(jnp.mean(inputs * inputs, axis=-1, keepdims=True) + EPSILON)
    normed = (inputs * scale_in * norm_gain).astype(jnp.bfloat16)
    projected = jnp.dot(normed, w_in_full, preferred_element_type=jnp.float32).astype(jnp.bfloat16)
    gate_z = projected[:, :DI].astype(jnp.float32)
    conv_in = projected[:, DI : DI + CHAN]
    dt_raw = projected[:, DI + CHAN :].astype(jnp.float32)
    first_row = lax.axis_index("seq") * length
    id_row = jnp.concatenate([jnp.full((CONV - 1,), -1, jnp.int32), segment_ids[0]], axis=0)
    ids_pad = lax.dynamic_slice_in_dim(id_row, first_row, length + CONV - 1)
    ids_own = ids_pad[CONV - 1 :]
    left_edge = passed_along(conv_in[length - (CONV - 1) :], "seq", 1)
    padded = jnp.concatenate([left_edge, conv_in], axis=0).astype(jnp.float32)
    kernel = conv_full.astype(jnp.float32)
    conv_out = jnp.zeros((length, CHAN), jnp.float32) + bias_full.astype(jnp.float32)
    same_docs = []
    for offset in range(CONV):
        same_doc = (ids_pad[offset : offset + length] == ids_own).astype(jnp.float32)
        same_docs.append(same_doc)
        conv_out = conv_out + kernel[offset] * padded[offset : offset + length] * same_doc[:, None]
    activated = jax.nn.silu(conv_out)
    blocks = length // SPAN
    x_heads = activated[:, :DI].reshape(blocks, SPAN, HEADS, HEADDIM)
    b_rows = activated[:, DI : DI + STATE].reshape(blocks, SPAN, STATE)
    c_rows = activated[:, DI + STATE :].reshape(blocks, SPAN, STATE)
    dt_bias_f = dt_bias_full.astype(jnp.float32)
    decay_rate = jnp.exp(a_log_full.astype(jnp.float32))
    step_flat = jax.nn.softplus(dt_raw + dt_bias_f)
    step_size = step_flat.reshape(blocks, SPAN, HEADS)
    log_decay = (-step_flat * decay_rate).reshape(blocks, SPAN, HEADS)
    ids_blocks = ids_own.reshape(blocks, SPAN)
    before_ids = ids_pad[CONV - 2 : CONV - 2 + length : SPAN]
    causal_mask, keep_flag, same_last = block_masks(ids_blocks, before_ids)

    def state_part(heads_in, rows_b, steps_in, decay_in):
        return local_states(heads_in, rows_b, steps_in, decay_in, same_last, keep_flag)

    (fresh_state, passing, total_state, total_decay), state_pull = jax.vjp(
        state_part, x_heads, b_rows, step_size, log_decay
    )

    def pass_forward(turn_index, received):
        return passed_along(
            (total_state + total_decay[:, None, None] * received).astype(jnp.bfloat16), "seq", 1
        ).astype(jnp.float32)

    incoming = lax.fori_loop(0, lax.axis_size("seq") - 1, pass_forward, jnp.zeros_like(total_state))

    def output_part(
        heads_in, rows_b, rows_c, steps_in, decay_in, fresh_in, passing_in, incoming_in
    ):
        return local_output(
            heads_in, rows_b, rows_c, steps_in, decay_in, incoming_in, causal_mask, keep_flag
        )

    ssd_out, output_pull = jax.vjp(
        output_part, x_heads, b_rows, c_rows, step_size, log_decay, fresh_state, passing, incoming
    )
    skip_heads = skip_full.astype(jnp.float32)
    y_full = (ssd_out + skip_heads[:, None] * x_heads).reshape(length, DI)
    silu_z = jax.nn.silu(gate_z)
    gated = y_full * silu_z
    scale_out = lax.rsqrt(jnp.mean(gated * gated, axis=-1, keepdims=True) + EPSILON)
    gate_gain = gate_full.astype(jnp.float32)
    normed_out = (gated * scale_out * gate_gain).astype(jnp.bfloat16)
    branch = jnp.dot(normed_out, w_out_full, preferred_element_type=jnp.float32)
    layer_out = (inputs + branch).astype(jnp.bfloat16)[None]
    grad_out = cotangent[0]
    d_w_out = lax.dot_general(
        normed_out, grad_out, (((0,), (0,)), ((), ())), preferred_element_type=jnp.float32
    )
    d_normed_out = lax.dot_general(
        grad_out, w_out_full, (((1,), (1,)), ((), ())), preferred_element_type=jnp.float32
    )
    d_gate_w = jnp.sum(d_normed_out * gated * scale_out, axis=0)
    along_out = d_normed_out * gate_gain
    cube_out = scale_out * scale_out * scale_out
    d_gated = scale_out * along_out - gated * cube_out * jnp.mean(
        along_out * gated, axis=-1, keepdims=True
    )
    d_y = d_gated * silu_z
    sig_z = jax.nn.sigmoid(gate_z)
    d_gate_z = d_gated * y_full * sig_z * (1.0 + gate_z * (1.0 - sig_z))
    d_ssd = d_y.reshape(blocks, SPAN, HEADS, HEADDIM)
    d_skip_grad = jnp.sum(d_ssd * x_heads, axis=(0, 1, 3))
    dx_out, db_out, dc_out, dstep_out, ddecay_out, d_fresh, d_passing, d_incoming = output_pull(
        d_ssd
    )

    def pass_backward(turn_index, received):
        return passed_along(d_incoming + total_decay[:, None, None] * received, "seq", -1)

    d_total = lax.fori_loop(0, lax.axis_size("seq") - 1, pass_backward, jnp.zeros_like(d_incoming))
    d_total_decay = jnp.sum(d_total * incoming, axis=(1, 2))
    dx_state, db_state, dstep_state, ddecay_state = state_pull(
        (d_fresh, d_passing, d_total, d_total_decay)
    )
    d_x = dx_out + dx_state + skip_heads[:, None] * d_ssd
    d_b = db_out + db_state
    d_log = (ddecay_out + ddecay_state).reshape(length, HEADS)
    d_step = (dstep_out + dstep_state).reshape(length, HEADS) - d_log * decay_rate
    d_a_log = -jnp.sum(d_log * step_flat, axis=0) * decay_rate
    d_dt_raw = d_step * jax.nn.sigmoid(dt_raw + dt_bias_f)
    d_dt_bias = jnp.sum(d_dt_raw, axis=0)
    d_act = jnp.concatenate(
        [d_x.reshape(length, DI), d_b.reshape(length, STATE), dc_out.reshape(length, STATE)], axis=1
    )
    sig_conv = jax.nn.sigmoid(conv_out)
    d_conv = d_act * sig_conv * (1.0 + conv_out * (1.0 - sig_conv))
    d_conv_b = jnp.sum(d_conv, axis=0)
    kernel_rows = []
    d_padded = jnp.zeros((length + CONV - 1, CHAN), jnp.float32)
    for offset in range(CONV):
        masked = d_conv * same_docs[offset][:, None]
        kernel_rows.append(jnp.sum(masked * padded[offset : offset + length], axis=0))
        d_padded = d_padded + jnp.pad(
            kernel[offset] * masked, ((offset, CONV - 1 - offset), (0, 0))
        )
    d_kernel = jnp.stack(kernel_rows)
    d_edge = passed_along(shortened(d_padded[: CONV - 1]), "seq", -1)
    d_conv_in = d_padded[CONV - 1 :] + jnp.pad(d_edge, ((length - (CONV - 1), 0), (0, 0)))
    d_projected = jnp.concatenate([d_gate_z, d_conv_in, d_dt_raw], axis=1).astype(jnp.bfloat16)
    d_normed = lax.dot_general(
        d_projected, w_in_full, (((1,), (1,)), ((), ())), preferred_element_type=jnp.float32
    )
    d_norm_w = jnp.sum(d_normed * inputs * scale_in, axis=0)
    along_in = d_normed * norm_gain
    cube_in = scale_in * scale_in * scale_in
    d_inputs = (
        scale_in * along_in
        - inputs * cube_in * jnp.mean(along_in * inputs, axis=-1, keepdims=True)
        + grad_out.astype(jnp.float32)
    )
    d_w_in = lax.dot_general(
        normed, d_projected, (((0,), (0,)), ((), ())), preferred_element_type=jnp.float32
    )
    weight_grads = (
        d_w_in,
        d_w_out,
        d_kernel,
        d_conv_b,
        d_a_log,
        d_dt_bias,
        d_skip_grad,
        d_norm_w,
        d_gate_w,
    )
    shares = tuple(
        (
            lax.psum_scatter(weight_grads[0], "fsdp", scatter_dimension=0, tiled=True),
            lax.psum_scatter(weight_grads[1], "fsdp", scatter_dimension=0, tiled=True),
            lax.psum_scatter(weight_grads[2], "fsdp", scatter_dimension=1, tiled=True),
            lax.psum_scatter(weight_grads[3], "fsdp", scatter_dimension=0, tiled=True),
            lax.psum_scatter(weight_grads[4], "fsdp", scatter_dimension=0, tiled=True),
            lax.psum_scatter(weight_grads[5], "fsdp", scatter_dimension=0, tiled=True),
            lax.psum_scatter(weight_grads[6], "fsdp", scatter_dimension=0, tiled=True),
            lax.psum_scatter(weight_grads[7], "fsdp", scatter_dimension=0, tiled=True),
            lax.psum_scatter(weight_grads[8], "fsdp", scatter_dimension=0, tiled=True),
        )
    )
    totals = lax.psum(shares, "seq")
    return (layer_out, d_inputs[None]) + tuple(totals)


def solution(mesh):
    return jax.shard_map(
        on_device,
        mesh=mesh,
        in_specs=(
            P("fsdp", "seq", None),
            P("fsdp", None),
            P("fsdp", "seq", None),
            P("fsdp", None),
            P("fsdp", None),
            P(None, "fsdp"),
            P("fsdp"),
            P("fsdp"),
            P("fsdp"),
            P("fsdp"),
            P("fsdp"),
            P("fsdp"),
        ),
        out_specs=(
            P("fsdp", "seq", None),
            P("fsdp", "seq", None),
            P("fsdp", None),
            P("fsdp", None),
            P(None, "fsdp"),
            P("fsdp"),
            P("fsdp"),
            P("fsdp"),
            P("fsdp"),
            P("fsdp"),
            P("fsdp"),
        ),
        check_vma=False,
    )
```

profile of v0, /device:TPU:0, one launch (start us, length us, event | category | flops | bytes accessed | tf_op | source)
XLA Modules:
  0.0 1851.0 jit_solution(16285410717219535761)
XLA Ops:
  9.6 13.5 all-gather.1
  23.2 13.2 all-gather
  40.1 30.4 %all-reduce.20 = (bf16[3328]{0:T(1024)(128)(2,1)S(1)}, bf16[48]{0:T(256)(128)(2,1)S(1)}, bf16[48]{0:T(256)(128)(2,1)S(1)}, bf16[48]{0:T(256)(128)(2,1)S(1)}) all-reduce(bf16[3328]{0:T(1024)(128)(2,1)S(1)} %dynamic-update-slice, bf16[48]{0:T(256)(128)(2,1)S(1)} %dynamic-update-slice.2, ...), channel_id=1, replica_groups=mesh['seq'=8,'fsdp'=4] {'fsdp'}, use_global_device_ids=true, to_apply=%add.7 | all-reduce | flops 3472 | bytes 13888
  74.6 30.3 %all-gather.2 = bf16[4,1,768]{2,1,0:T(2,128)(2,1)S(1)} all-gather(bf16[1,1,768]{2,1,0:T(2,128)(2,1)S(1)} %reshape.689), channel_id=1, replica_groups=mesh['seq'=8,'fsdp'=4] {'fsdp'}, dimensions={0}, use_global_device_ids=true | all-gather | bytes 7680 | tf_op jit(solution)/shard_map/all_gather | solution.py:94
  107.8 243.6 %all-gather.6.cloned.1.call-done = bf16[1536,6448]{0,1:T(8,128)(2,1)} async-done(((bf16[384,6448]{0,1:T(8,128)(2,1)}), bf16[1536,6448]{0,1:T(8,128)(2,1)}) %all-gather.6.cloned.1.call-update) | async-done | bytes 19808272 | tf_op jit(solution)/shard_map/all_gather | solution.py:86
  351.4 9.9 convolution_convert_fusion
  385.7 4.7 fusion.27
  394.2 3.6 copy.162
  399.8 5.7 fusion.61
  405.6 122.4 %while.22 = (s32[]{:T(128)}, f32[48,64,128]{2,1,0:T(8,128)}, f32[1,48]{1,0:T(1,128)}, f32[48,64,128]{2,1,0:T(8,128)}, s32[]{:T(128)}, /*index=5*/s32[]{:T(128)}) while((s32[]{:T(128)}, f32[48,64,128]{2,1,0:T(8,128)}, f32[1,48]{1,0:T(1,128)}, f32[48,64,128]{2,1,0:T(8,128)}, s32[]{:T(128)}, /*index=5*/s32[]{:T(128)}) %tuple.82), condition=%wide.region_4.5_spmd.clone, body=%wide.region_3.4_spmd.clone.sunk | while | flops 1966083 | bytes 9437495 | solution.py:155
  408.1 3.9 collective-permute-start.1
  418.9 9.9 collective-permute-start.1
  432.5 3.0 fusion.137
  435.6 12.3 collective-permute-start.1
  454.6 12.3 collective-permute-start.1
  473.8 12.3 collective-permute-start.1
  492.8 12.3 collective-permute-start.1
  511.9 12.3 collective-permute-start.1
  528.1 4.2 fusion.94
  532.4 16.3 fusion.35
  548.7 3.5 copy.171
  552.2 3.6 multiply_reduce_fusion.10
  557.5 8.0 fusion.76
  568.2 3.8 copy.174
  572.0 8.4 multiply_reduce_fusion.6
  580.4 5.6 multiply_reduce_fusion.7
  586.1 3.9 copy.173
  590.0 5.0 mul.702
  595.0 3.6 copy.175
  598.6 5.6 fusion.92
  605.6 173.4 %while.21 = (s32[]{:T(128)}, f32[48,64,128]{2,1,0:T(8,128)}, f32[1,48]{1,0:T(1,128)}, f32[48,64,128]{2,1,0:T(8,128)}, s32[]{:T(128)}) while((s32[]{:T(128)}, f32[48,64,128]{2,1,0:T(8,128)}, f32[1,48]{1,0:T(1,128)}, f32[48,64,128]{2,1,0:T(8,128)}, s32[]{:T(128)}) %tuple.102), condition=%wide.region_8.9_spmd, body=%wide.region_7.8_spmd.sunk | while | flops 786434 | bytes 11010341 | solution.py:201
  605.6 3.3 multiply_add_fusion.4
  610.2 13.1 collective-permute-done
  623.3 3.3 multiply_add_fusion.4
  628.0 22.6 %collective-permute-done = f32[48,64,128]{2,1,0:T(8,128)} collective-permute-done((f32[48,64,128]{2,1,0:T(8,128)}, f32[48,64,128]{2,1,0:T(8,128)}, u32[]{:S(2)}, u32[]{:S(2)}) %collective-permute-start) | collective-permute-done | bytes 1572896 | tf_op jit(solution)/shard_map/while/body/eval_jaxpr/ppermute | solution.py:20
  650.6 3.3 multiply_add_fusion.4
  655.2 21.0 %collective-permute-done = f32[48,64,128]{2,1,0:T(8,128)} collective-permute-done((f32[48,64,128]{2,1,0:T(8,128)}, f32[48,64,128]{2,1,0:T(8,128)}, u32[]{:S(2)}, u32[]{:S(2)}) %collective-permute-start) | collective-permute-done | bytes 1572896 | tf_op jit(solution)/shard_map/while/body/eval_jaxpr/ppermute | solution.py:20
  676.2 3.3 multiply_add_fusion.4
  680.8 21.1 %collective-permute-done = f32[48,64,128]{2,1,0:T(8,128)} collective-permute-done((f32[48,64,128]{2,1,0:T(8,128)}, f32[48,64,128]{2,1,0:T(8,128)}, u32[]{:S(2)}, u32[]{:S(2)}) %collective-permute-start) | collective-permute-done | bytes 1572896 | tf_op jit(solution)/shard_map/while/body/eval_jaxpr/ppermute | solution.py:20
  701.9 3.3 multiply_add_fusion.4
  706.5 21.0 %collective-permute-done = f32[48,64,128]{2,1,0:T(8,128)} collective-permute-done((f32[48,64,128]{2,1,0:T(8,128)}, f32[48,64,128]{2,1,0:T(8,128)}, u32[]{:S(2)}, u32[]{:S(2)}) %collective-permute-start) | collective-permute-done | bytes 1572896 | tf_op jit(solution)/shard_map/while/body/eval_jaxpr/ppermute | solution.py:20
  727.6 3.6 multiply_add_fusion.4
  732.4 20.8 %collective-permute-done = f32[48,64,128]{2,1,0:T(8,128)} collective-permute-done((f32[48,64,128]{2,1,0:T(8,128)}, f32[48,64,128]{2,1,0:T(8,128)}, u32[]{:S(2)}, u32[]{:S(2)}) %collective-permute-start) | collective-permute-done | bytes 1572896 | tf_op jit(solution)/shard_map/while/body/eval_jaxpr/ppermute | solution.py:20
  753.2 3.4 multiply_add_fusion.4
  758.0 21.0 %collective-permute-done = f32[48,64,128]{2,1,0:T(8,128)} collective-permute-done((f32[48,64,128]{2,1,0:T(8,128)}, f32[48,64,128]{2,1,0:T(8,128)}, u32[]{:S(2)}, u32[]{:S(2)}) %collective-permute-start) | collective-permute-done | bytes 1572896 | tf_op jit(solution)/shard_map/while/body/eval_jaxpr/ppermute | solution.py:20
  779.0 7.4 fusion.37
  787.9 23.3 %fusion.10 = (f32[48,256]{1,0:T(8,128)}, f32[48,256]{1,0:T(8,128)}, f32[48,256]{1,0:T(8,128)}, f32[256,256]{1,0:T(8,128)}) fusion(f32[48,256]{1,0:T(8,128)} %copy.166, f32[256,256]{1,0:T(8,128)} %get-tuple-element.160, f32[48,256]{1,0:T(8,128)} %bitcast_add_fusion.7, f32[256,256]{1,0:T(8,128)} %fusion.101, pred[256,256]{1,0:T(8,128)(4,1)} %get-tuple-element.159, ...), kind=kOutput, calls=%fused_computation.15 | convolution fusion | flops 2463002624 | bytes 7389184 | tf_op jit(solution)/shard_map/transpose(jvp(chts,cshp->cthp))/dot_general | solution.py:63
  814.3 4.2 multiply_reduce_fusion.8
  827.2 3.8 reduce-window.26
  835.4 3.8 reduce-window.24
  841.8 15.3 fusion.34
  857.2 3.7 copy.180
  862.6 7.5 convolution_bitcast_fusion
  871.7 6.5 fusion.72
  878.3 4.8 multiply_reduce_fusion.5
  895.1 11.3 collective-permute-done.3
  908.6 17.6 fusion.64
  928.9 661.6 %reduce-scatter.6.cloned.1.call-done = f32[384,6448]{0,1:T(8,128)} async-done(((f32[1536,6448]{0,1:T(8,128)}), f32[384,6448]{0,1:T(8,128)}) %reduce-scatter.6.cloned.1.call-update) | async-done | bytes 9904144 | tf_op jit(solution)/shard_map/reduce_scatter | solution.py:258
  1593.8 7.5 fusion.43
  1601.4 9.9 fusion.57
  1611.4 22.4 %all-reduce.19 = (f32[3328]{0:T(1024)S(1)}, f32[48]{0:T(128)S(1)}, f32[48]{0:T(128)S(1)}, f32[48]{0:T(128)S(1)}, f32[1536]{0:T(1024)S(1)}, /*index=5*/f32[3072]{0:T(1024)S(1)}) all-reduce(f32[3328]{0:T(1024)S(1)} %copy-done.36, f32[48]{0:T(128)S(1)} %negate_multiply_fusion.1, ...), channel_id=5, replica_groups=mesh['seq'=8,'fsdp'=4] {'fsdp'}, use_global_device_ids=true, to_apply=%region_33.34.clone | all-reduce | flops 8080 | bytes 64640
  1637.0 24.0 %all-reduce.17 = (f32[4,832]{1,0:T(4,128)}, f32[832]{0:T(1024)}, f32[12]{0:T(128)}, f32[12]{0:T(128)}, f32[12]{0:T(128)}, /*index=5*/f32[384]{0:T(512)}, f32[768]{0:T(1024)}) all-reduce(f32[4,832]{1,0:T(4,128)S(1)} %copy.204, f32[832]{0:T(1024)S(1)} %dynamic-slice.5, ...), channel_id=1, replica_groups=mesh['seq'=8,'fsdp'=4] {'seq'}, use_global_device_ids=true, to_apply=%region_31.32 | all-reduce | flops 5348 | bytes 42784 | tf_op jit(solution)/shard_map/psum | solution.py:269
  1661.0 172.3 %all-reduce.23.cloned.1.call-done = (f32[384,6448]{0,1:T(8,128)}, f32[768,1536]{1,0:T(8,128)}) async-done(((f32[384,6448]{0,1:T(8,128)}, f32[768,1536]{1,0:T(8,128)}), (f32[384,6448]{0,1:T(8,128)}, f32[768,1536]{1,0:T(8,128)})) %all-reduce.23.cloned.1.call-update) | async-done | bytes 14622736 | tf_op jit(solution)/shard_map/psum | solution.py:269
  1833.2 8.5 copy.227
  (311 shorter events, 146.7 us)
Async XLA Ops:
  7.2 29.9 %copy-start.69 = (u32[32]{0:T(128)S(1)}, u32[32]{0:T(128)}, u32[]{:S(2)}) copy-start(u32[32]{0:T(128)} %constant.79) | copy-start | bytes 388
  7.2 15.9 copy-start.64
  7.2 31.8 %copy-start.76 = (bf16[12]{0:T(256)(128)(2,1)S(1)}, bf16[12]{0:T(256)(128)(2,1)}, u32[]{:S(2)}) copy-start(bf16[12]{0:T(256)(128)(2,1)} %param.23) | copy-start | bytes 76
  7.2 32.1 %copy-start.77 = (bf16[12]{0:T(256)(128)(2,1)S(1)}, bf16[12]{0:T(256)(128)(2,1)}, u32[]{:S(2)}) copy-start(bf16[12]{0:T(256)(128)(2,1)} %param.24) | copy-start | bytes 76
  7.2 32.3 %copy-start.78 = (bf16[12]{0:T(256)(128)(2,1)S(1)}, bf16[12]{0:T(256)(128)(2,1)}, u32[]{:S(2)}) copy-start(bf16[12]{0:T(256)(128)(2,1)} %param.25) | copy-start | bytes 76
  7.3 32.6 %copy-start.70 = (bf16[832]{0:T(1024)(128)(2,1)S(1)}, bf16[832]{0:T(1024)(128)(2,1)}, u32[]{:S(2)}) copy-start(bf16[832]{0:T(1024)(128)(2,1)} %param.22) | copy-start | bytes 4996
  7.3 67.3 %copy-start.71 = (bf16[768]{0:T(1024)(128)(2,1)S(1)}, bf16[768]{0:T(1024)(128)(2,1)}, u32[]{:S(2)}) copy-start(bf16[768]{0:T(1024)(128)(2,1)} %param.27) | copy-start | bytes 4612
  7.3 98.3 %copy-start.12 = (bf16[1,256,1536]{2,1,0:T(8,128)(2,1)S(1)}, bf16[1,256,1536]{2,1,0:T(8,128)(2,1)}, u32[]{:S(2)}) copy-start(bf16[1,256,1536]{2,1,0:T(8,128)(2,1)} %param.16) | copy-start | bytes 2359300
  7.3 344.1 %all-gather.6.cloned.1.call-start = ((), (), s32[]{:S(2)}) async-start(), calls=%async_computation.3 | async-start | bytes 24760320 | tf_op jit(solution)/shard_map/all_gather | solution.py:86
  8.0 564.0 %all-gather.8.cloned.1.call-start = ((), (), s32[]{:S(2)}) async-start(), calls=%async_computation.4 | async-start | bytes 11796480 | tf_op jit(solution)/shard_map/all_gather | solution.py:87
  8.8 920.1 %reduce-scatter.8.cloned.1.call-start = ((), (), s32[]{:S(2)}) async-start(), calls=%async_computation.6 | async-start | bytes 23592960 | tf_op jit(solution)/shard_map/reduce_scatter | solution.py:259
  70.4 281.0 %copy-start.79 = (bf16[48]{0:T(256)(128)(2,1)}, bf16[48]{0:T(256)(128)(2,1)S(1)}, u32[]{:S(2)}) copy-start(bf16[48]{0:T(256)(128)(2,1)S(1)} %get-tuple-element.123) | copy-start | bytes 292
  73.5 301.8 %copy-start.47 = (f32[256]{0:T(256)}, f32[256]{0:T(256)S(1)}, u32[]{:S(2)}) copy-start(f32[256]{0:T(256)S(1)} %get-tuple-element.150) | copy-start | bytes 3076
  351.4 10.0 copy-start.58
  351.4 10.0 copy-start.72
  351.4 17.2 copy-start.55
  361.3 22.6 %copy-start.11 = (bf16[256,6448]{1,0:T(8,128)(2,1)}, bf16[256,6448]{1,0:T(8,128)(2,1)S(1)}, u32[]{:S(2)}) copy-start(bf16[256,6448]{1,0:T(8,128)(2,1)S(1)} %convolution_convert_fusion) | copy-start | bytes 9904132
  365.8 18.1 collective-permute-start.2
  370.3 13.6 copy-start.20
  373.8 10.1 copy-start.61
  408.1 5.3 collective-permute-start.1
  418.9 11.2 collective-permute-start.1
  435.6 13.6 collective-permute-start.1
  454.6 13.7 collective-permute-start.1
  473.8 13.6 collective-permute-start.1
  492.8 13.6 collective-permute-start.1
  511.9 13.6 collective-permute-start.1
  532.3 16.4 copy-start.9
  565.5 1025.0 %reduce-scatter.6.cloned.1.call-start = ((), (), s32[]{:S(2)}) async-start(), calls=%async_computation.5 | async-start | bytes 49520640 | tf_op jit(solution)/shard_map/reduce_scatter | solution.py:258
  572.0 8.4 copy-start.3
  572.0 8.4 copy-start.5
  572.0 8.4 copy-start.7
  572.0 8.4 copy-start.51
  572.0 8.4 copy-start.68
  608.9 14.4 collective-permute-start
  626.7 23.9 %collective-permute-start = (f32[48,64,128]{2,1,0:T(8,128)}, f32[48,64,128]{2,1,0:T(8,128)}, u32[]{:S(2)}, u32[]{:S(2)}) collective-permute-start(f32[48,64,128]{2,1,0:T(8,128)} %multiply_add_fusion.4), channel_id=1, source_target_pairs={{4,0},{8,4},{12,8},{16,12},{20,16},{24,20},{28,24},{5,1},{9,5},{13... | collective-permute-start | bytes 4718600 | tf_op jit(solution)/shard_map/while/body/eval_jaxpr/ppermute | solution.py:20
  653.9 22.3 %collective-permute-start = (f32[48,64,128]{2,1,0:T(8,128)}, f32[48,64,128]{2,1,0:T(8,128)}, u32[]{:S(2)}, u32[]{:S(2)}) collective-permute-start(f32[48,64,128]{2,1,0:T(8,128)} %multiply_add_fusion.4), channel_id=1, source_target_pairs={{4,0},{8,4},{12,8},{16,12},{20,16},{24,20},{28,24},{5,1},{9,5},{13... | collective-permute-start | bytes 4718600 | tf_op jit(solution)/shard_map/while/body/eval_jaxpr/ppermute | solution.py:20
  679.5 22.4 %collective-permute-start = (f32[48,64,128]{2,1,0:T(8,128)}, f32[48,64,128]{2,1,0:T(8,128)}, u32[]{:S(2)}, u32[]{:S(2)}) collective-permute-start(f32[48,64,128]{2,1,0:T(8,128)} %multiply_add_fusion.4), channel_id=1, source_target_pairs={{4,0},{8,4},{12,8},{16,12},{20,16},{24,20},{28,24},{5,1},{9,5},{13... | collective-permute-start | bytes 4718600 | tf_op jit(solution)/shard_map/while/body/eval_jaxpr/ppermute | solution.py:20
  705.2 22.3 %collective-permute-start = (f32[48,64,128]{2,1,0:T(8,128)}, f32[48,64,128]{2,1,0:T(8,128)}, u32[]{:S(2)}, u32[]{:S(2)}) collective-permute-start(f32[48,64,128]{2,1,0:T(8,128)} %multiply_add_fusion.4), channel_id=1, source_target_pairs={{4,0},{8,4},{12,8},{16,12},{20,16},{24,20},{28,24},{5,1},{9,5},{13... | collective-permute-start | bytes 4718600 | tf_op jit(solution)/shard_map/while/body/eval_jaxpr/ppermute | solution.py:20
  731.1 22.1 %collective-permute-start = (f32[48,64,128]{2,1,0:T(8,128)}, f32[48,64,128]{2,1,0:T(8,128)}, u32[]{:S(2)}, u32[]{:S(2)}) collective-permute-start(f32[48,64,128]{2,1,0:T(8,128)} %multiply_add_fusion.4), channel_id=1, source_target_pairs={{4,0},{8,4},{12,8},{16,12},{20,16},{24,20},{28,24},{5,1},{9,5},{13... | collective-permute-start | bytes 4718600 | tf_op jit(solution)/shard_map/while/body/eval_jaxpr/ppermute | solution.py:20
  756.7 22.3 %collective-permute-start = (f32[48,64,128]{2,1,0:T(8,128)}, f32[48,64,128]{2,1,0:T(8,128)}, u32[]{:S(2)}, u32[]{:S(2)}) collective-permute-start(f32[48,64,128]{2,1,0:T(8,128)} %multiply_add_fusion.4), channel_id=1, source_target_pairs={{4,0},{8,4},{12,8},{16,12},{20,16},{24,20},{28,24},{5,1},{9,5},{13... | collective-permute-start | bytes 4718600 | tf_op jit(solution)/shard_map/while/body/eval_jaxpr/ppermute | solution.py:20
  860.9 9.3 copy-start.23
  860.9 10.8 copy-start.1
  860.9 10.8 copy-start.27
  862.6 15.6 copy-start.10
  870.2 8.0 copy-start.8
  870.2 8.0 copy-start.44
  870.2 8.0 copy-start.45
  870.2 8.0 copy-start.46
  884.3 8.2 copy-start.49
  884.3 8.2 copy-start.60
  884.3 8.2 copy-start.63
  886.0 20.4 %collective-permute-start.3 = (bf16[3,3328]{1,0:T(4,128)(2,1)}, bf16[3,3328]{1,0:T(4,128)(2,1)}, u32[]{:S(2)}, u32[]{:S(2)}) collective-permute-start(bf16[3,3328]{1,0:T(4,128)(2,1)} %slice.240), channel_id=1, source_target_pairs={{4,0},{8,4},{12,8},{16,12},{20,16},{24,20},{28,24},{5,1},{9,5},{13... | collective-permute-start | bytes 59912 | tf_op jit(solution)/shard_map/ppermute | solution.py:20
  926.2 709.6 %reduce-scatter.10.cloned.1.call-start = ((), (), s32[]{:S(2)}) async-start(), calls=%async_computation.7 | async-start | bytes 2129920
  928.8 904.4 %all-reduce.23.cloned.1.call-start = ((), (), s32[]{:S(2)}) async-start(), calls=%async_computation.8 | async-start | bytes 29245440 | tf_op jit(solution)/shard_map/psum | solution.py:269
  1593.8 7.5 copy-start.13
  1593.8 7.5 copy-start.15
  1601.4 10.0 copy-start.36
  1601.4 10.0 copy-start.53
  1601.4 10.0 copy-start.73
  1601.4 32.8 %copy-start.14 = (bf16[1,256,1536]{2,1,0:T(8,128)(2,1)S(1)}, bf16[1,256,1536]{2,1,0:T(8,128)(2,1)}, u32[]{:S(2)}) copy-start(bf16[1,256,1536]{2,1,0:T(8,128)(2,1)} %param.16) | copy-start | bytes 2359300
  1601.4 32.8 %copy-start.19 = (bf16[1,256,1536]{2,1,0:T(8,128)(2,1)S(1)}, bf16[1,256,1536]{2,1,0:T(8,128)(2,1)}, u32[]{:S(2)}) copy-start(bf16[1,256,1536]{2,1,0:T(8,128)(2,1)} %param.18) | copy-start | bytes 2359300
  1601.4 32.8 %copy-start.67 = (f32[256]{0:T(256)S(1)}, f32[256]{0:T(256)}, u32[]{:S(2)}) copy-start(f32[256]{0:T(256)} %get-tuple-element.155) | copy-start | bytes 3076
  1833.2 8.5 copy-start.17
  (40 other events, 125.9 us)
Sparse Core Ops, SparseCore 0:
  9.7 341.6 all-gather.5
  353.0 165.5 all-gather.7
  565.6 328.2 reduce-scatter.7
  926.4 664.1 reduce-scatter.5
  1593.4 40.8 reduce-scatter.9
  1638.4 194.8 all-reduce.22
where the time goes:
time: 1860 us; the launch traced here: 1850 us
  waiting for transfers between devices  1240 us (67%)
  matrix products  158 us (8%)
  blocking collectives  134 us (7%)
  other arithmetic  131 us (7%)
  starting transfers between devices  88.3 us (5%)
  local copies, waits for them, and re-layouts  79.2 us (4%)
  between operations  19.7 us (1%)
    reduce_scatter x1, waiting for transfers between devices, on_device(): lax.psum_scatter(weight_grads[0], 'fsdp', scatter_dimension=0, tiled=True)  662 us
    all_gather x1, waiting for transfers between devices, on_device(): lax.all_gather(w_in, 'fsdp', axis=0, tiled=True)  244 us
    psum x1, waiting for transfers between devices, on_device(): totals = lax.psum(shares, 'seq')  172 us
    ppermute x16, waiting for transfers between devices, passed_along(): lax.ppermute(value, axis, [(source, source + steps) for source in range(f...  161 us
    ppermute x16, starting transfers between devices, passed_along(): lax.ppermute(value, axis, [(source, source + steps) for source in range(f...  88.1 us
    dot_general x3, matrix products, local_output(): jnp.einsum('chts,cshp->cthp', mixing, x_heads, precision=HIGHEST)  54.9 us
    unnamed x2, blocking collectives  52.7 us
  transfers between devices with their start and end apart: 22, of which 18 were waited for; matrix products, arithmetic and copies ran while one was open for 19% of the time, Pallas kernels for 0%

commit v1 on v0

--- a/solution.py
+++ b/solution.py
@@ -12,6 +12,29 @@
 CHAN = 3328
 EPSILON = 1e-05
 HIGHEST = lax.Precision.HIGHEST
+
+
+def in_order(tiles, dim):
+    shape = list(tiles.shape[1:])
+    shape[dim] *= tiles.shape[0]
+    return jnp.moveaxis(tiles, 0, dim).reshape(shape)
+
+
+def grow_blocks(x, axis):
+    count, position = (lax.axis_size(axis), lax.axis_index(axis))
+    blocks, bit = (x[None], 1)
+    while bit < count:
+        partner_block = lax.ppermute(blocks, axis, [(i, i ^ bit) for i in range(count)])
+        low = position & bit == 0
+        blocks = jnp.concatenate(
+            [jnp.where(low, blocks, partner_block), jnp.where(low, partner_block, blocks)]
+        )
+        bit *= 2
+    return blocks
+
+
+def doubled_up(array, axis, dim):
+    return in_order(grow_blocks(array, axis), dim)
 
 
 def passed_along(value, axis, steps):
@@ -83,7 +106,7 @@
     gate_w,
 ):
     gathered = (
-        lax.all_gather(w_in, "fsdp", axis=0, tiled=True),
+        doubled_up(w_in, "fsdp", 0),
         lax.all_gather(w_out, "fsdp", axis=0, tiled=True),
         lax.all_gather(conv_w, "fsdp", axis=1, tiled=True),
         lax.all_gather(conv_b, "fsdp", axis=0, tiled=True),

time: 1860 us -> 2320 us (1.25)
  blocking collectives: 134 us -> 664 us
  waiting for transfers between devices: 1240 us -> 1100 us
  other arithmetic: 131 us -> 166 us
  local copies, waits for them, and re-layouts: 79.2 us -> 105 us
    all_gather x1, blocking collectives: 13.5 us -> 583 us  [on_device(): lax.all_gather(norm_w, 'fsdp', axis=0, tiled=True)]
    all_gather x1 -> x0, waiting for transfers between devices: 244 us -> none  [on_device(): lax.all_gather(w_in, 'fsdp', axis=0, tiled=True)]
    ppermute x0 -> x2, waiting for transfers between devices: none -> 107 us  [grow_blocks(): lax.ppermute(blocks, axis, [(i, i ^ bit) for i in range(count)])]
    concatenate x0 -> x1, local copies, waits for them, and re-layouts: none -> 25.3 us  [grow_blocks(): jnp.concatenate([jnp.where(low, blocks, partner_block), jnp.where(low, pa...]
  transfers between devices with their start and end apart: 22 -> 23, of which waited for: 18 -> 18; matrix products, arithmetic and copies ran while one was open for 19% -> 17% of each run, Pallas kernels for 0% -> 0%
where the time goes in v1:
time: 2320 us; the launch traced here: 2310 us
  waiting for transfers between devices  1100 us (47%)
  blocking collectives  664 us (29%)
  other arithmetic  166 us (7%)
  matrix products  162 us (7%)
  local copies, waits for them, and re-layouts  105 us (5%)
  starting transfers between devices  93.8 us (4%)
    reduce_scatter x1, waiting for transfers between devices, on_device(): lax.psum_scatter(weight_grads[0], 'fsdp', scatter_dimension=0, tiled=True)  663 us
    all_gather x1, blocking collectives, on_device(): lax.all_gather(norm_w, 'fsdp', axis=0, tiled=True)  583 us
    psum x1, waiting for transfers between devices, on_device(): totals = lax.psum(shares, 'seq')  172 us
    ppermute x16, waiting for transfers between devices, passed_along(): lax.ppermute(value, axis, [(source, source + steps) for source in range(f...  161 us
    ppermute x2, waiting for transfers between devices, grow_blocks(): lax.ppermute(blocks, axis, [(i, i ^ bit) for i in range(count)])  107 us
    ppermute x16, starting transfers between devices, passed_along(): lax.ppermute(value, axis, [(source, source + steps) for source in range(f...  87.8 us
    dot_general x3, matrix products, local_output(): jnp.einsum('chts,cshp->cthp', mixing, x_heads, precision=HIGHEST)  54.3 us
  transfers between devices with their start and end apart: 23, of which 18 were waited for; matrix products, arithmetic and copies ran while one was open for 17% of the time, Pallas kernels for 0%

profile of v1, /device:TPU:0, one launch (start us, length us, event | category | flops | bytes accessed | tf_op | source)
XLA Modules:
  0.0 2312.2 jit_solution(12500215099880276874)
XLA Ops:
  10.3 107.1 %collective-permute-done.2 = bf16[1,384,6448]{1,2,0:T(8,128)(2,1)} collective-permute-done((bf16[1,384,6448]{1,2,0:T(8,128)(2,1)}, bf16[1,384,6448]{1,2,0:T(8,128)(2,1)}, u32[]{:S(2)}, u32[]{:S(2)}) %collective-permute-start.2) | collective-permute-done | bytes 4952096 | tf_op jit(solution)/shard_map/ppermute | solution.py:27
  117.4 8.6 broadcast_select_fusion.3
  126.1 9.0 pad_maximum_fusion.1
  138.7 582.7 %all-gather.1 = bf16[4,1,384]{2,1,0:T(2,128)(2,1)S(1)} all-gather(bf16[1,1,384]{2,1,0:T(2,128)(2,1)S(1)} %reshape.705), channel_id=1, replica_groups=mesh['seq'=8,'fsdp'=4] {'fsdp'}, dimensions={0}, use_global_device_ids=true | all-gather | bytes 3840 | tf_op jit(solution)/shard_map/all_gather | solution.py:116
  721.4 13.1 all-gather
  738.2 8.7 all-reduce.20
  751.2 13.0 all-gather.2
  767.1 8.1 broadcast_select_fusion.1
  775.2 8.5 pad_maximum_fusion
  783.7 25.3 %copy.166 = bf16[4,384,6448]{2,1,0:T(8,128)(2,1)} copy(bf16[4,384,6448]{1,2,0:T(8,128)(2,1)} %pad_maximum_fusion) | data formatting | bytes 39616512 | tf_op jit(solution)/shard_map/concatenate | solution.py:29
  809.0 12.7 convolution_convert_fusion
  845.5 4.7 fusion.27
  854.0 3.5 copy.168
  859.6 5.7 fusion.68
  865.4 122.9 %while.22 = (s32[]{:T(128)}, f32[48,64,128]{2,1,0:T(8,128)}, f32[1,48]{1,0:T(1,128)}, f32[48,64,128]{2,1,0:T(8,128)}, s32[]{:T(128)}, /*index=5*/s32[]{:T(128)}) while((s32[]{:T(128)}, f32[48,64,128]{2,1,0:T(8,128)}, f32[1,48]{1,0:T(1,128)}, f32[48,64,128]{2,1,0:T(8,128)}, s32[]{:T(128)}, /*index=5*/s32[]{:T(128)}) %tuple.84), condition=%wide.region_4.5_spmd.clone, body=%wide.region_3.4_spmd.clone.sunk | while | flops 1966083 | bytes 9437495 | solution.py:178
  867.9 4.4 collective-permute-start.1
  879.2 9.8 collective-permute-start.1
  895.8 12.3 collective-permute-start.1
  914.9 12.3 collective-permute-start.1
  934.0 12.3 collective-permute-start.1
  953.1 12.3 collective-permute-start.1
  972.2 12.3 collective-permute-start.1
  988.3 4.2 fusion.106
  992.6 16.0 fusion.35
  1008.6 3.5 copy.177
  1012.2 3.6 multiply_reduce_fusion.10
  1017.5 8.0 fusion.86
  1028.2 4.0 copy.180
  1032.2 8.4 multiply_reduce_fusion.6
  1040.7 5.6 multiply_reduce_fusion.7
  1046.3 4.1 copy.179
  1050.4 5.0 mul.713
  1055.5 3.6 copy.181
  1059.0 5.6 fusion.104
  1066.0 172.5 %while.21 = (s32[]{:T(128)}, f32[48,64,128]{2,1,0:T(8,128)}, f32[1,48]{1,0:T(1,128)}, f32[48,64,128]{2,1,0:T(8,128)}, s32[]{:T(128)}) while((s32[]{:T(128)}, f32[48,64,128]{2,1,0:T(8,128)}, f32[1,48]{1,0:T(1,128)}, f32[48,64,128]{2,1,0:T(8,128)}, s32[]{:T(128)}) %tuple.102), condition=%wide.region_8.9_spmd, body=%wide.region_7.8_spmd.sunk | while | flops 786434 | bytes 11010341 | solution.py:224
  1070.7 12.9 collective-permute-done
  1083.6 3.3 multiply_add_fusion.4
  1088.2 22.0 collective-permute-done
  1114.8 21.0 collective-permute-done
  1140.5 21.0 collective-permute-done
  1161.5 3.4 multiply_add_fusion.4
  1166.2 21.0 collective-permute-done
  1187.2 3.3 multiply_add_fusion.4
  1191.8 21.0 collective-permute-done
  1217.5 21.0 collective-permute-done
  1238.5 7.4 fusion.37
  1247.5 23.0 fusion.10
  1273.6 4.2 multiply_reduce_fusion.8
  1287.3 3.8 reduce-window.26
  1295.5 3.8 reduce-window.24
  1302.0 15.3 fusion.34
  1317.4 3.9 copy.186
  1323.1 7.5 convolution_bitcast_fusion
  1332.1 6.5 fusion.79
  1338.7 4.7 multiply_reduce_fusion.5
  1355.5 11.3 collective-permute-done.5
  1369.0 17.6 fusion.71
  1389.3 662.9 %reduce-scatter.6.cloned.1.call-done = f32[384,6448]{0,1:T(8,128)} async-done(((f32[1536,6448]{0,1:T(8,128)}), f32[384,6448]{0,1:T(8,128)}) %reduce-scatter.6.cloned.1.call-update) | async-done | bytes 9904144 | tf_op jit(solution)/shard_map/reduce_scatter | solution.py:281
  2055.3 7.4 fusion.43
  2062.7 11.1 fusion.62
  2073.9 22.1 all-reduce.19
  2099.2 24.0 %all-reduce.17 = (f32[4,832]{1,0:T(4,128)}, f32[832]{0:T(1024)}, f32[12]{0:T(128)}, f32[12]{0:T(128)}, f32[12]{0:T(128)}, /*index=5*/f32[384]{0:T(512)}, f32[768]{0:T(1024)}) all-reduce(f32[4,832]{1,0:T(4,128)S(1)} %copy.210, f32[832]{0:T(1024)S(1)} %dynamic-slice.5, ...), channel_id=1, replica_groups=mesh['seq'=8,'fsdp'=4] {'seq'}, use_global_device_ids=true, to_apply=%region_31.32 | all-reduce | flops 5348 | bytes 42784 | tf_op jit(solution)/shard_map/psum | solution.py:292
  2123.2 171.6 %all-reduce.23.cloned.1.call-done = (f32[384,6448]{0,1:T(8,128)}, f32[768,1536]{1,0:T(8,128)}) async-done(((f32[384,6448]{0,1:T(8,128)}, f32[768,1536]{1,0:T(8,128)}), (f32[384,6448]{0,1:T(8,128)}, f32[768,1536]{1,0:T(8,128)})) %all-reduce.23.cloned.1.call-update) | async-done | bytes 14622736 | tf_op jit(solution)/shard_map/psum | solution.py:292
  2294.8 8.5 copy.233
  (293 shorter events, 168.2 us)
Async XLA Ops:
  7.2 1025.0 %all-gather.5.cloned.1.call-start = ((), (), s32[]{:S(2)}) async-start(), calls=%async_computation.3 | async-start | bytes 11796480 | tf_op jit(solution)/shard_map/all_gather | solution.py:110
  7.2 110.2 %collective-permute-start.2 = (bf16[1,384,6448]{1,2,0:T(8,128)(2,1)}, bf16[1,384,6448]{1,2,0:T(8,128)(2,1)}, u32[]{:S(2)}, u32[]{:S(2)}) collective-permute-start(bf16[1,384,6448]{1,2,0:T(8,128)(2,1)} %bitcast.324), channel_id=1, source_target_pairs={{0,1},{1,0},{2,3},{3,2},{4,5},{5,4},{6,7},{7,6},{8,9},{9,8},{10,11... | collective-permute-start | bytes 14856200 | tf_op jit(solution)/shard_map/ppermute | solution.py:27
  126.1 11.9 copy-start.47
  126.1 12.6 copy-start.62
  126.1 595.4 %copy-start.52 = (bf16[4,832]{1,0:T(4,128)(2,1)S(1)}, bf16[4,832]{1,0:T(4,128)(2,1)}, u32[]{:S(2)}) copy-start(bf16[4,832]{1,0:T(4,128)(2,1)} %param.21) | copy-start | bytes 19972
  126.1 609.2 %copy-start.57 = (u32[32]{0:T(128)S(1)}, u32[32]{0:T(128)}, u32[]{:S(2)}) copy-start(u32[32]{0:T(128)} %constant.86) | copy-start | bytes 388
  126.1 611.1 %copy-start.64 = (bf16[12]{0:T(256)(128)(2,1)S(1)}, bf16[12]{0:T(256)(128)(2,1)}, u32[]{:S(2)}) copy-start(bf16[12]{0:T(256)(128)(2,1)} %param.23) | copy-start | bytes 76
  126.1 611.4 %copy-start.65 = (bf16[12]{0:T(256)(128)(2,1)S(1)}, bf16[12]{0:T(256)(128)(2,1)}, u32[]{:S(2)}) copy-start(bf16[12]{0:T(256)(128)(2,1)} %param.24) | copy-start | bytes 76
  126.1 611.6 %copy-start.66 = (bf16[12]{0:T(256)(128)(2,1)S(1)}, bf16[12]{0:T(256)(128)(2,1)}, u32[]{:S(2)}) copy-start(bf16[12]{0:T(256)(128)(2,1)} %param.25) | copy-start | bytes 76
  126.1 611.9 %copy-start.58 = (bf16[832]{0:T(1024)(128)(2,1)S(1)}, bf16[832]{0:T(1024)(128)(2,1)}, u32[]{:S(2)}) copy-start(bf16[832]{0:T(1024)(128)(2,1)} %param.22) | copy-start | bytes 4996
  126.1 625.0 %copy-start.59 = (bf16[768]{0:T(1024)(128)(2,1)S(1)}, bf16[768]{0:T(1024)(128)(2,1)}, u32[]{:S(2)}) copy-start(bf16[768]{0:T(1024)(128)(2,1)} %param.27) | copy-start | bytes 4612
  135.1 629.9 %copy-start.12 = (bf16[1,256,1536]{2,1,0:T(8,128)(2,1)S(1)}, bf16[1,256,1536]{2,1,0:T(8,128)(2,1)}, u32[]{:S(2)}) copy-start(bf16[1,256,1536]{2,1,0:T(8,128)(2,1)} %param.16) | copy-start | bytes 2359300
  135.1 632.1 %collective-permute-start.3 = (bf16[2,384,6448]{1,2,0:T(8,128)(2,1)}, bf16[2,384,6448]{1,2,0:T(8,128)(2,1)}, u32[]{:S(2)}, u32[]{:S(2)}) collective-permute-start(bf16[2,384,6448]{1,2,0:T(8,128)(2,1)} %pad_maximum_fusion.1), channel_id=1, source_target_pairs={{0,2},{1,3},{2,0},{3,1},{4,6},{5,7},{6,4},{7,5},{8,10},{9,11},{10,... | collective-permute-start | bytes 29712392 | tf_op jit(solution)/shard_map/ppermute | solution.py:27
  137.9 1251.4 %reduce-scatter.8.cloned.1.call-start = ((), (), s32[]{:S(2)}) async-start(), calls=%async_computation.5 | async-start | bytes 23592960 | tf_op jit(solution)/shard_map/reduce_scatter | solution.py:282
  746.9 28.3 %copy-start.67 = (bf16[48]{0:T(256)(128)(2,1)}, bf16[48]{0:T(256)(128)(2,1)S(1)}, u32[]{:S(2)}) copy-start(bf16[48]{0:T(256)(128)(2,1)S(1)} %get-tuple-element.123) | copy-start | bytes 292
  750.1 85.0 %copy-start.39 = (f32[256]{0:T(256)}, f32[256]{0:T(256)S(1)}, u32[]{:S(2)}) copy-start(f32[256]{0:T(256)S(1)} %get-tuple-element.154) | copy-start | bytes 3076
  809.0 12.8 copy-start.48
  809.0 12.8 copy-start.60
  809.0 19.5 copy-start.46
  821.7 22.0 copy-start.11
  826.2 17.5 collective-permute-start.4
  830.1 13.6 copy-start.17
  833.6 10.1 copy-start.50
  867.9 5.8 collective-permute-start.1
  879.2 11.2 collective-permute-start.1
  895.8 13.6 collective-permute-start.1
  914.9 13.6 collective-permute-start.1
  934.0 13.6 collective-permute-start.1
  953.1 13.6 collective-permute-start.1
  972.2 13.6 collective-permute-start.1
  992.6 16.1 copy-start.9
  1025.5 1026.7 %reduce-scatter.6.cloned.1.call-start = ((), (), s32[]{:S(2)}) async-start(), calls=%async_computation.4 | async-start | bytes 49520640 | tf_op jit(solution)/shard_map/reduce_scatter | solution.py:281
  1032.2 8.4 copy-start.3
  1032.2 8.4 copy-start.5
  1032.2 8.4 copy-start.7
  1032.2 8.4 copy-start.42
  1032.2 8.4 copy-start.56
  1069.4 14.2 collective-permute-start
  1086.9 23.3 %collective-permute-start = (f32[48,64,128]{2,1,0:T(8,128)}, f32[48,64,128]{2,1,0:T(8,128)}, u32[]{:S(2)}, u32[]{:S(2)}) collective-permute-start(f32[48,64,128]{2,1,0:T(8,128)} %multiply_add_fusion.4), channel_id=1, source_target_pairs={{4,0},{8,4},{12,8},{16,12},{20,16},{24,20},{28,24},{5,1},{9,5},{13... | collective-permute-start | bytes 4718600 | tf_op jit(solution)/shard_map/while/body/eval_jaxpr/ppermute | solution.py:43
  1113.5 22.3 collective-permute-start
  1139.2 22.3 collective-permute-start
  1165.0 22.3 collective-permute-start
  1190.5 22.3 collective-permute-start
  1216.2 22.3 collective-permute-start
  1321.3 9.3 copy-start.18
  1321.3 10.8 copy-start.1
  1321.3 10.8 copy-start.19
  1323.1 15.6 copy-start.10
  1330.6 8.0 copy-start.8
  1330.6 8.0 copy-start.36
  1330.6 8.0 copy-start.37
  1344.7 8.2 copy-start.40
  1344.7 8.2 copy-start.49
  1344.7 8.2 copy-start.51
  1346.4 20.4 collective-permute-start.5
  1386.6 711.4 %reduce-scatter.10.cloned.1.call-start = ((), (), s32[]{:S(2)}) async-start(), calls=%async_computation.6 | async-start | bytes 2129920
  1389.2 905.5 %all-reduce.23.cloned.1.call-start = ((), (), s32[]{:S(2)}) async-start(), calls=%async_computation.7 | async-start | bytes 29245440 | tf_op jit(solution)/shard_map/psum | solution.py:292
  2062.7 11.2 copy-start.28
  2062.7 11.2 copy-start.44
  2062.7 11.2 copy-start.61
  2062.7 33.7 %copy-start.13 = (bf16[1,256,1536]{2,1,0:T(8,128)(2,1)S(1)}, bf16[1,256,1536]{2,1,0:T(8,128)(2,1)}, u32[]{:S(2)}) copy-start(bf16[1,256,1536]{2,1,0:T(8,128)(2,1)} %param.16) | copy-start | bytes 2359300
  2062.7 33.7 %copy-start.16 = (bf16[1,256,1536]{2,1,0:T(8,128)(2,1)S(1)}, bf16[1,256,1536]{2,1,0:T(8,128)(2,1)}, u32[]{:S(2)}) copy-start(bf16[1,256,1536]{2,1,0:T(8,128)(2,1)} %param.18) | copy-start | bytes 2359300
  2062.7 33.7 %copy-start.55 = (f32[256]{0:T(256)S(1)}, f32[256]{0:T(256)}, u32[]{:S(2)}) copy-start(f32[256]{0:T(256)} %get-tuple-element.159) | copy-start | bytes 3076
  2294.7 8.5 copy-start.14
  (29 other events, 98.7 us)
Sparse Core Ops, SparseCore 0:
  138.0 441.2 all-gather.4
  1025.6 328.9 reduce-scatter.7
  1386.8 665.3 reduce-scatter.5
  2055.0 40.8 reduce-scatter.9
  2100.0 194.6 all-reduce.22
